TPU v7x, 32 devices: a whole 2x2x4 slice. The times are simulated.
32 devices in a mesh: section: 4 (over x, core), tp: 8 (over z, y).
Axes of the slice: x: 2, y: 2, z: 4, core: 2. Of those that a mesh axis runs over, the one named last changes fastest.
Arguments:
- layer_inputs: bfloat16 [8, 512, 4096], P('section', None, 'tp'), may hold values from -6 to 6
- weights: bfloat16 [8, 4096, 4096], P('section', 'tp'), may hold values from -0.046875 to 0.046875
- input_basis: bfloat16 [8, 4096, 64], P('section', 'tp'), may hold values from -0.09375 to 0.09375
- output_basis: bfloat16 [8, 4096, 32], P('section', 'tp'), may hold values from -0.09375 to 0.09375
- queries: bfloat16 [8, 512, 2048], P('section', 'tp'), may hold values from -0.00390625 to 0.00390625
- top_cotangent: bfloat16 [512, 4096], replicated, may hold values from -6 to 6
- sequence_example: int32 [4], replicated, may hold values from 0 to 1
Outputs:
- scores: float32 [2, 512], P(None, 'tp')
All inputs are finite; a program needn't handle non-finite values.
Results may differ from a plain program's by a relative error of at most 0.0094.
Values may be sent and summed in bfloat16 or wider, within the bound.
A program may use at most 64 MiB of HBM per device.

v0:
```python
import jax
import jax.numpy as jnp
from jax import lax
from jax.sharding import PartitionSpec as P

SEQLEN = 128
SEQ_MB = 1
MB = 4
EXAMPLES = 2


def from_behind(value, axis, by):
    size = lax.axis_size(axis)
    pairs = [(i, i + by) for i in range(size) if 0 <= i + by < size]
    return lax.ppermute(value, axis, pairs)


def silu_parts(values):
    floats = values.astype(jnp.float32)
    logistic = jax.nn.sigmoid(floats)
    return ((floats * logistic).astype(jnp.bfloat16), logistic * (1.0 + floats * (1.0 - logistic)))


def contract_columns(portion, matrix):
    return lax.dot_general(
        portion, matrix, (((1,), (1,)), ((), ())), preferred_element_type=jnp.float32
    )


def outer_rows(out_feats, in_feats):
    joined = out_feats[:, :, :, None] * in_feats[:, :, None, :]
    return joined.reshape(joined.shape[0], joined.shape[1], -1)


def shards(
    layer_inputs, weights, input_basis, output_basis, queries, top_cotangent, sequence_example
):
    section_count = lax.axis_size("section")
    section_rank = lax.axis_index("section")
    tp_rank = lax.axis_index("tp")
    width_local = layer_inputs.shape[2]
    total_tokens = layer_inputs.shape[1]
    block_rows = SEQ_MB * SEQLEN
    activated, slopes = silu_parts(layer_inputs)
    partial_in = jnp.einsum(
        "ltd,ldr->tlr", activated, input_basis, preferred_element_type=jnp.float32
    )
    in_feats = lax.psum(partial_in.reshape(total_tokens, -1), "tp").reshape(partial_in.shape)
    example_index = jnp.arange(EXAMPLES, dtype=jnp.int32)
    is_top = section_rank == section_count - 1

    def fold_upper(portion):
        return contract_columns(portion, weights[1])

    def fold_lower(portion):
        return contract_columns(portion, weights[0])

    def tick(tick_index, state):
        outgoing, grads, stored = state
        micro_index = tick_index - (section_count - 1 - section_rank)
        valid = (micro_index >= 0) & (micro_index < MB)
        micro_clip = jnp.clip(micro_index, 0, MB - 1)
        first_row = micro_clip * block_rows
        slope_block = lax.dynamic_slice_in_dim(slopes, first_row, block_rows, 1)
        received = from_behind(outgoing, "section", -1)
        top_block = lax.dynamic_slice(
            top_cotangent, (first_row, tp_rank * width_local), (block_rows, width_local)
        )
        upper_own = jnp.where(is_top, top_block, received)
        upper_branch = fold_upper(lax.all_gather(upper_own, "tp", axis=1, tiled=True))
        middle_own = (upper_own.astype(jnp.float32) + slope_block[1] * upper_branch).astype(
            jnp.bfloat16
        )
        lower_branch = fold_lower(lax.all_gather(middle_own, "tp", axis=1, tiled=True))
        lower_own = (middle_own.astype(jnp.float32) + slope_block[0] * lower_branch).astype(
            jnp.bfloat16
        )
        cotangents = jnp.stack([middle_own, upper_own], 0)
        partial_out = jnp.einsum(
            "lrd,ldk->rlk", cotangents, output_basis, preferred_element_type=jnp.float32
        )
        out_feats = lax.psum(partial_out.reshape(block_rows, -1), "tp").reshape(partial_out.shape)
        in_block = lax.dynamic_slice_in_dim(in_feats, first_row, block_rows, 0)
        block_examples = jnp.repeat(
            lax.dynamic_slice_in_dim(sequence_example, micro_clip * SEQ_MB, SEQ_MB, 0), SEQLEN
        )
        selector = (example_index[:, None] == block_examples[None, :]).astype(
            jnp.float32
        ) * valid.astype(jnp.float32)
        grads = grads + jnp.einsum(
            "er,rlk->lek",
            selector,
            outer_rows(out_feats, in_block),
            precision=lax.Precision.HIGHEST,
        )
        return (lower_own, grads, stored)

    outgoing_init = jnp.zeros((block_rows, width_local), jnp.bfloat16)
    grads_init = jnp.zeros((2, EXAMPLES, queries.shape[2]), jnp.float32)
    stored_init = jnp.zeros((1,), jnp.bfloat16)
    final_out, grads, stored = lax.fori_loop(
        0, MB + section_count - 1, tick, (outgoing_init, grads_init, stored_init)
    )
    layer_scores = jnp.einsum(
        "lek,lqk->eq", grads, queries.astype(jnp.float32), precision=lax.Precision.HIGHEST
    )
    return lax.psum(layer_scores, "section")


def solution(mesh):
    placed = (
        P("section", None, "tp"),
        P("section", "tp", None),
        P("section", "tp", None),
        P("section", "tp", None),
        P("section", "tp", None),
        P(),
        P(),
    )
    return jax.shard_map(
        shards, mesh=mesh, in_specs=placed, out_specs=P(None, "tp"), check_vma=False
    )
```

profile of v0, /device:TPU:0, one launch (start us, length us, event | category | flops | bytes accessed | tf_op | source)
XLA Modules:
  0.0 749.2 jit_solution(505250659360147819)
XLA Ops:
  6.5 2.7 convolution_bitcast_fusion.2
  9.3 1.9 fusion.28
  11.2 73.2 %all-reduce.2.cloned.1.call-done = f32[512,2,64]{0,2,1:T(8,128)} async-done(((f32[512,2,64]{0,2,1:T(8,128)}), f32[512,2,64]{0,2,1:T(8,128)}) %all-reduce.2.cloned.1.call-update) | async-done | bytes 262160 | tf_op jit(solution)/shard_map/psum | solution.py:48
  84.5 651.5 %while.18 = (s32[]{:T(128)}, bf16[128,512]{1,0:T(8,128)(2,1)S(1)}, f32[2,2,2048]{2,1,0:T(2,128)S(1)}, pred[]{:T(512)}, s32[]{:T(128)}, /*index=5*/bf16[512,4096]...) while((s32[]{:T(128)}, bf16[128,512]{1,0:T(8,128)(2,1)S(1)}, ...), condition=%wide.region_3.4_spmd.clone, body=%wide.region_1.3_spmd.clone.sunk | while | flops 1096048640 | bytes 25756184 | solution.py:101
  85.8 1.9 collective-permute-done
  89.4 40.3 %all-gather.3.cloned.1.call-done = bf16[128,4096]{1,0:T(8,128)(2,1)} async-done(((bf16[128,512]{1,0:T(8,128)(2,1)}), bf16[128,4096]{1,0:T(8,128)(2,1)}) %all-gather.3.cloned.1.call-update) | async-done | bytes 1048592 | tf_op jit(solution)/shard_map/while/body/eval_jaxpr/all_gather | solution.py:70
  129.7 4.7 add_convert_fusion.4
  137.5 35.6 %psum.31 = f32[128,2,32]{0,2,1:T(8,128)S(1)} all-reduce(f32[128,2,32]{0,2,1:T(8,128)S(1)} %convolution_bitcast_fusion.5), channel_id=1, replica_groups=mesh['section'=4,'tp'=8] {'tp'}, use_global_device_ids=true, to_apply=%region_2.2 | all-reduce | flops 8192 | bytes 65536 | tf_op jit(solution)/shard_map/while/body/eval_jaxpr/psum | solution.py:82
  173.3 1.9 fusion.56
  175.3 4.0 add_convert_fusion.5
  180.7 1.9 collective-permute-done
  184.3 38.2 %all-gather.3.cloned.1.call-done = bf16[128,4096]{1,0:T(8,128)(2,1)} async-done(((bf16[128,512]{1,0:T(8,128)(2,1)}), bf16[128,4096]{1,0:T(8,128)(2,1)}) %all-gather.3.cloned.1.call-update) | async-done | bytes 1048592 | tf_op jit(solution)/shard_map/while/body/eval_jaxpr/all_gather | solution.py:70
  222.5 4.7 add_convert_fusion.4
  230.3 35.6 %psum.31 = f32[128,2,32]{0,2,1:T(8,128)S(1)} all-reduce(f32[128,2,32]{0,2,1:T(8,128)S(1)} %convolution_bitcast_fusion.5), channel_id=1, replica_groups=mesh['section'=4,'tp'=8] {'tp'}, use_global_device_ids=true, to_apply=%region_2.2 | all-reduce | flops 8192 | bytes 65536 | tf_op jit(solution)/shard_map/while/body/eval_jaxpr/psum | solution.py:82
  266.1 1.9 fusion.56
  268.0 4.0 add_convert_fusion.5
  273.5 1.9 collective-permute-done
  277.1 38.2 %all-gather.3.cloned.1.call-done = bf16[128,4096]{1,0:T(8,128)(2,1)} async-done(((bf16[128,512]{1,0:T(8,128)(2,1)}), bf16[128,4096]{1,0:T(8,128)(2,1)}) %all-gather.3.cloned.1.call-update) | async-done | bytes 1048592 | tf_op jit(solution)/shard_map/while/body/eval_jaxpr/all_gather | solution.py:70
  315.3 4.7 add_convert_fusion.4
  323.0 35.6 %psum.31 = f32[128,2,32]{0,2,1:T(8,128)S(1)} all-reduce(f32[128,2,32]{0,2,1:T(8,128)S(1)} %convolution_bitcast_fusion.5), channel_id=1, replica_groups=mesh['section'=4,'tp'=8] {'tp'}, use_global_device_ids=true, to_apply=%region_2.2 | all-reduce | flops 8192 | bytes 65536 | tf_op jit(solution)/shard_map/while/body/eval_jaxpr/psum | solution.py:82
  358.9 1.9 fusion.56
  360.8 4.0 add_convert_fusion.5
  366.3 1.9 collective-permute-done
  368.2 1.6 dynamic-slice_select_fusion.2
  369.8 38.2 %all-gather.3.cloned.1.call-done = bf16[128,4096]{1,0:T(8,128)(2,1)} async-done(((bf16[128,512]{1,0:T(8,128)(2,1)}), bf16[128,4096]{1,0:T(8,128)(2,1)}) %all-gather.3.cloned.1.call-update) | async-done | bytes 1048592 | tf_op jit(solution)/shard_map/while/body/eval_jaxpr/all_gather | solution.py:70
  408.0 4.7 add_convert_fusion.4
  415.8 35.6 %psum.31 = f32[128,2,32]{0,2,1:T(8,128)S(1)} all-reduce(f32[128,2,32]{0,2,1:T(8,128)S(1)} %convolution_bitcast_fusion.5), channel_id=1, replica_groups=mesh['section'=4,'tp'=8] {'tp'}, use_global_device_ids=true, to_apply=%region_2.2 | all-reduce | flops 8192 | bytes 65536 | tf_op jit(solution)/shard_map/while/body/eval_jaxpr/psum | solution.py:82
  451.6 1.9 fusion.56
  453.6 4.0 add_convert_fusion.5
  459.0 1.9 collective-permute-done
  462.6 38.2 %all-gather.3.cloned.1.call-done = bf16[128,4096]{1,0:T(8,128)(2,1)} async-done(((bf16[128,512]{1,0:T(8,128)(2,1)}), bf16[128,4096]{1,0:T(8,128)(2,1)}) %all-gather.3.cloned.1.call-update) | async-done | bytes 1048592 | tf_op jit(solution)/shard_map/while/body/eval_jaxpr/all_gather | solution.py:70
  500.8 4.7 add_convert_fusion.4
  508.6 35.6 %psum.31 = f32[128,2,32]{0,2,1:T(8,128)S(1)} all-reduce(f32[128,2,32]{0,2,1:T(8,128)S(1)} %convolution_bitcast_fusion.5), channel_id=1, replica_groups=mesh['section'=4,'tp'=8] {'tp'}, use_global_device_ids=true, to_apply=%region_2.2 | all-reduce | flops 8192 | bytes 65536 | tf_op jit(solution)/shard_map/while/body/eval_jaxpr/psum | solution.py:82
  544.4 1.9 fusion.56
  546.3 4.0 add_convert_fusion.5
  551.8 1.9 collective-permute-done
  555.4 38.2 %all-gather.3.cloned.1.call-done = bf16[128,4096]{1,0:T(8,128)(2,1)} async-done(((bf16[128,512]{1,0:T(8,128)(2,1)}), bf16[128,4096]{1,0:T(8,128)(2,1)}) %all-gather.3.cloned.1.call-update) | async-done | bytes 1048592 | tf_op jit(solution)/shard_map/while/body/eval_jaxpr/all_gather | solution.py:70
  593.6 4.7 add_convert_fusion.4
  601.3 35.6 %psum.31 = f32[128,2,32]{0,2,1:T(8,128)S(1)} all-reduce(f32[128,2,32]{0,2,1:T(8,128)S(1)} %convolution_bitcast_fusion.5), channel_id=1, replica_groups=mesh['section'=4,'tp'=8] {'tp'}, use_global_device_ids=true, to_apply=%region_2.2 | all-reduce | flops 8192 | bytes 65536 | tf_op jit(solution)/shard_map/while/body/eval_jaxpr/psum | solution.py:82
  637.2 1.9 fusion.56
  639.1 4.0 add_convert_fusion.5
  644.6 1.9 collective-permute-done
  648.1 38.2 %all-gather.3.cloned.1.call-done = bf16[128,4096]{1,0:T(8,128)(2,1)} async-done(((bf16[128,512]{1,0:T(8,128)(2,1)}), bf16[128,4096]{1,0:T(8,128)(2,1)}) %all-gather.3.cloned.1.call-update) | async-done | bytes 1048592 | tf_op jit(solution)/shard_map/while/body/eval_jaxpr/all_gather | solution.py:70
  686.3 4.7 add_convert_fusion.4
  694.1 35.6 %psum.31 = f32[128,2,32]{0,2,1:T(8,128)S(1)} all-reduce(f32[128,2,32]{0,2,1:T(8,128)S(1)} %convolution_bitcast_fusion.5), channel_id=1, replica_groups=mesh['section'=4,'tp'=8] {'tp'}, use_global_device_ids=true, to_apply=%region_2.2 | all-reduce | flops 8192 | bytes 65536 | tf_op jit(solution)/shard_map/while/body/eval_jaxpr/psum | solution.py:82
  729.9 1.9 fusion.56
  731.9 4.0 add_convert_fusion.5
  736.4 6.2 psum.28
  (129 shorter events, 43.3 us)
Async XLA Ops:
  6.5 729.4 %copy-start = (bf16[2,64,2048]{2,1,0:T(8,128)(2,1)S(1)}, bf16[2,64,2048]{2,1,0:T(8,128)(2,1)}, u32[]{:S(2)}) copy-start(bf16[2,64,2048]{2,1,0:T(8,128)(2,1)} %param.13) | copy-start | bytes 1572868
  6.5 77.9 %all-reduce.2.cloned.1.call-start = ((), (), s32[]{:S(2)}) async-start(), calls=%async_computation | async-start | bytes 524288 | tf_op jit(solution)/shard_map/psum | solution.py:48
  9.2 75.2 %copy-start.3 = (bf16[2,512,32]{1,2,0:T(8,128)(2,1)S(1)}, bf16[2,512,32]{1,2,0:T(8,128)(2,1)}, u32[]{:S(2)}) copy-start(bf16[2,512,32]{1,2,0:T(8,128)(2,1)} %param.12) | copy-start | bytes 196612
  9.2 75.2 %copy-start.4 = (s32[4]{0:T(128)S(1)}, s32[4]{0:T(128)}, u32[]{:S(2)}) copy-start(s32[4]{0:T(128)} %param.15) | copy-start | bytes 52
  84.5 45.3 %all-gather.3.cloned.1.call-start = ((), (), s32[]{:S(2)}) async-start(), calls=%async_computation.1 | async-start | bytes 1179648 | tf_op jit(solution)/shard_map/while/body/eval_jaxpr/all_gather | solution.py:70
  84.5 3.2 collective-permute-start
  89.3 85.9 %all-gather.5.cloned.1.call-start = ((), (), s32[]{:S(2)}) async-start(), calls=%async_computation.2 | async-start | bytes 1179648 | tf_op jit(solution)/shard_map/while/body/eval_jaxpr/all_gather | solution.py:74
  129.7 6.7 copy-start.1
  173.1 2.2 copy-start.2
  179.3 43.2 %all-gather.3.cloned.1.call-start = ((), (), s32[]{:S(2)}) async-start(), calls=%async_computation.1 | async-start | bytes 1179648 | tf_op jit(solution)/shard_map/while/body/eval_jaxpr/all_gather | solution.py:70
  179.4 3.2 collective-permute-start
  184.3 83.7 %all-gather.5.cloned.1.call-start = ((), (), s32[]{:S(2)}) async-start(), calls=%async_computation.2 | async-start | bytes 1179648 | tf_op jit(solution)/shard_map/while/body/eval_jaxpr/all_gather | solution.py:74
  222.5 6.7 copy-start.1
  265.8 2.2 copy-start.2
  272.1 43.2 %all-gather.3.cloned.1.call-start = ((), (), s32[]{:S(2)}) async-start(), calls=%async_computation.1 | async-start | bytes 1179648 | tf_op jit(solution)/shard_map/while/body/eval_jaxpr/all_gather | solution.py:70
  272.2 3.2 collective-permute-start
  277.0 83.7 %all-gather.5.cloned.1.call-start = ((), (), s32[]{:S(2)}) async-start(), calls=%async_computation.2 | async-start | bytes 1179648 | tf_op jit(solution)/shard_map/while/body/eval_jaxpr/all_gather | solution.py:74
  315.3 6.7 copy-start.1
  358.6 2.2 copy-start.2
  364.9 43.2 %all-gather.3.cloned.1.call-start = ((), (), s32[]{:S(2)}) async-start(), calls=%async_computation.1 | async-start | bytes 1179648 | tf_op jit(solution)/shard_map/while/body/eval_jaxpr/all_gather | solution.py:70
  364.9 3.2 collective-permute-start
  369.8 83.7 %all-gather.5.cloned.1.call-start = ((), (), s32[]{:S(2)}) async-start(), calls=%async_computation.2 | async-start | bytes 1179648 | tf_op jit(solution)/shard_map/while/body/eval_jaxpr/all_gather | solution.py:74
  408.0 6.7 copy-start.1
  451.4 2.2 copy-start.2
  457.6 43.2 %all-gather.3.cloned.1.call-start = ((), (), s32[]{:S(2)}) async-start(), calls=%async_computation.1 | async-start | bytes 1179648 | tf_op jit(solution)/shard_map/while/body/eval_jaxpr/all_gather | solution.py:70
  457.7 3.2 collective-permute-start
  462.6 83.7 %all-gather.5.cloned.1.call-start = ((), (), s32[]{:S(2)}) async-start(), calls=%async_computation.2 | async-start | bytes 1179648 | tf_op jit(solution)/shard_map/while/body/eval_jaxpr/all_gather | solution.py:74
  500.8 6.7 copy-start.1
  544.1 2.2 copy-start.2
  550.4 43.2 %all-gather.3.cloned.1.call-start = ((), (), s32[]{:S(2)}) async-start(), calls=%async_computation.1 | async-start | bytes 1179648 | tf_op jit(solution)/shard_map/while/body/eval_jaxpr/all_gather | solution.py:70
  550.5 3.2 collective-permute-start
  555.3 83.7 %all-gather.5.cloned.1.call-start = ((), (), s32[]{:S(2)}) async-start(), calls=%async_computation.2 | async-start | bytes 1179648 | tf_op jit(solution)/shard_map/while/body/eval_jaxpr/all_gather | solution.py:74
  593.6 6.7 copy-start.1
  636.9 2.2 copy-start.2
  643.2 43.2 %all-gather.3.cloned.1.call-start = ((), (), s32[]{:S(2)}) async-start(), calls=%async_computation.1 | async-start | bytes 1179648 | tf_op jit(solution)/shard_map/while/body/eval_jaxpr/all_gather | solution.py:70
  643.2 3.2 collective-permute-start
  648.1 83.7 %all-gather.5.cloned.1.call-start = ((), (), s32[]{:S(2)}) async-start(), calls=%async_computation.2 | async-start | bytes 1179648 | tf_op jit(solution)/shard_map/while/body/eval_jaxpr/all_gather | solution.py:74
  686.3 6.7 copy-start.1
  729.7 2.2 copy-start.2
Sparse Core Ops, SparseCore 0:
  10.7 73.7 all-reduce.1
  89.5 40.2 all-gather.2
  134.6 38.5 all-gather.4
  184.4 38.0 all-gather.2
  227.3 38.5 all-gather.4
  277.2 38.0 all-gather.2
  320.1 38.5 all-gather.4
  369.9 38.0 all-gather.2
  412.9 38.5 all-gather.4
  462.7 38.0 all-gather.2
  505.6 38.5 all-gather.4
  555.5 38.0 all-gather.2
  598.4 38.5 all-gather.4
  648.2 38.0 all-gather.2
  691.2 38.5 all-gather.4
where the time goes:
time: 750 us; the launch traced here: 749 us
  waiting for transfers between devices  356 us (47%)
  blocking collectives  255 us (34%)
  matrix products  85.2 us (11%)
  other arithmetic  18.8 us (3%)
  between operations  13.1 us (2%)
  local copies, waits for them, and re-layouts  9.96 us (1%)
  starting transfers between devices  9.6 us (1%)
    all_gather x7, waiting for transfers between devices, tick(): lax.all_gather(upper_own, 'tp', axis=1, tiled=True)  269 us
    psum x7, blocking collectives, tick(): lax.psum(partial_out.reshape(block_rows, -1), 'tp')  249 us
    psum x1, waiting for transfers between devices, shards(): lax.psum(partial_in.reshape(total_tokens, -1), 'tp')  73.2 us
    dot_general x14, matrix products, contract_columns(): lax.dot_general(portion, matrix, (((1,), (1,)), ((), ())), preferred_elem...  61.2 us
  transfers between devices with their start and end apart: 22, of which 15 were waited for; matrix products, arithmetic and copies ran while one was open for 5% of the time, Pallas kernels for 0%

commit v1 on v0

--- a/solution.py
+++ b/solution.py
@@ -7,6 +7,11 @@
 SEQ_MB = 1
 MB = 4
 EXAMPLES = 2
+
+
+def add_all(value, name):
+    parts = lax.all_gather(value, name)
+    return jnp.sum(parts, axis=0)
 
 
 def from_behind(value, axis, by):
@@ -79,7 +84,7 @@
         partial_out = jnp.einsum(
             "lrd,ldk->rlk", cotangents, output_basis, preferred_element_type=jnp.float32
         )
-        out_feats = lax.psum(partial_out.reshape(block_rows, -1), "tp").reshape(partial_out.shape)
+        out_feats = add_all(partial_out.reshape(block_rows, -1), "tp").reshape(partial_out.shape)
         in_block = lax.dynamic_slice_in_dim(in_feats, first_row, block_rows, 0)
         block_examples = jnp.repeat(
             lax.dynamic_slice_in_dim(sequence_example, micro_clip * SEQ_MB, SEQ_MB, 0), SEQLEN

time: 750 us -> 754 us (level)
  waiting for transfers between devices: 356 us -> 387 us
  blocking collectives: 255 us -> 228 us
    psum x7 -> x0, blocking collectives: 249 us -> none  [tick(): lax.psum(partial_out.reshape(block_rows, -1), 'tp')]
    all_gather x0 -> x7, blocking collectives: none -> 222 us  [add_all(): parts = lax.all_gather(value, name)]
    all_gather x7, waiting for transfers between devices: 0.12 us -> 19.5 us  [tick(): lax.all_gather(middle_own, 'tp', axis=1, tiled=True)]
    all_gather x7, waiting for transfers between devices: 269 us -> 280 us  [tick(): lax.all_gather(upper_own, 'tp', axis=1, tiled=True)]
  transfers between devices with their start and end apart: 22 -> 22, of which waited for: 15 -> 22; matrix products, arithmetic and copies ran while one was open for 5% -> 5% of each run, Pallas kernels for 0% -> 0%
where the time goes in v1:
time: 754 us; the launch traced here: 752 us
  waiting for transfers between devices  387 us (51%)
  blocking collectives  228 us (30%)
  matrix products  85.2 us (11%)
  other arithmetic  18.9 us (3%)
  between operations  13.1 us (2%)
  local copies, waits for them, and re-layouts  9.96 us (1%)
  starting transfers between devices  9.6 us (1%)
    all_gather x7, waiting for transfers between devices, tick(): lax.all_gather(upper_own, 'tp', axis=1, tiled=True)  280 us
    all_gather x7, blocking collectives, add_all(): parts = lax.all_gather(value, name)  222 us
    psum x1, waiting for transfers between devices, shards(): lax.psum(partial_in.reshape(total_tokens, -1), 'tp')  73.2 us
    dot_general x14, matrix products, contract_columns(): lax.dot_general(portion, matrix, (((1,), (1,)), ((), ())), preferred_elem...  61.2 us
    all_gather x7, waiting for transfers between devices, tick(): lax.all_gather(middle_own, 'tp', axis=1, tiled=True)  19.5 us
  transfers between devices with their start and end apart: 22, of which 22 were waited for; matrix products, arithmetic and copies ran while one was open for 5% of the time, Pallas kernels for 0%

profile of v1, /device:TPU:0, one launch (start us, length us, event | category | flops | bytes accessed | tf_op | source)
XLA Modules:
  0.0 752.5 jit_solution(16859818776599766043)
XLA Ops:
  6.5 2.7 convolution_bitcast_fusion.1
  9.3 1.9 fusion.29
  11.2 73.2 %all-reduce.2.cloned.1.call-done = f32[512,2,64]{0,2,1:T(8,128)} async-done(((f32[512,2,64]{0,2,1:T(8,128)}), f32[512,2,64]{0,2,1:T(8,128)}) %all-reduce.2.cloned.1.call-update) | async-done | bytes 262160 | tf_op jit(solution)/shard_map/psum | solution.py:53
  84.5 654.7 %while.18 = (s32[]{:T(128)}, bf16[128,512]{1,0:T(8,128)(2,1)S(1)}, f32[2,2,2048]{2,1,0:T(2,128)S(1)}, pred[]{:T(512)}, s32[]{:T(128)}, /*index=5*/bf16[512,4096]...) while((s32[]{:T(128)}, bf16[128,512]{1,0:T(8,128)(2,1)S(1)}, ...), condition=%wide.region_3.4_spmd.clone, body=%wide.region_1.3_spmd.clone.sunk | while | flops 1096097792 | bytes 26280484 | solution.py:106
  85.8 1.9 collective-permute-done
  89.4 40.3 %all-gather.3.cloned.1.call-done = bf16[128,4096]{1,0:T(8,128)(2,1)} async-done(((bf16[128,512]{1,0:T(8,128)(2,1)}), bf16[128,4096]{1,0:T(8,128)(2,1)}) %all-gather.3.cloned.1.call-update) | async-done | bytes 1048592 | tf_op jit(solution)/shard_map/while/body/eval_jaxpr/all_gather | solution.py:75
  129.7 4.7 add_convert_fusion.4
  137.5 31.7 %all_gather.35 = f32[8,128,64]{1,2,0:T(8,128)S(1)} all-gather(f32[1,128,64]{1,2,0:T(8,128)S(1)} %bitcast.83), channel_id=1, replica_groups=mesh['section'=4,'tp'=8] {'tp'}, dimensions={0}, use_global_device_ids=true | all-gather | bytes 294912 | tf_op jit(solution)/shard_map/while/body/eval_jaxpr/all_gather | solution.py:13
  169.5 1.9 fusion.59
  171.4 2.8 all-gather.5.cloned.1.call-done
  174.2 4.0 add_convert_fusion.5
  179.6 1.9 collective-permute-done
  183.2 40.0 %all-gather.3.cloned.1.call-done = bf16[128,4096]{1,0:T(8,128)(2,1)} async-done(((bf16[128,512]{1,0:T(8,128)(2,1)}), bf16[128,4096]{1,0:T(8,128)(2,1)}) %all-gather.3.cloned.1.call-update) | async-done | bytes 1048592 | tf_op jit(solution)/shard_map/while/body/eval_jaxpr/all_gather | solution.py:75
  223.2 4.7 add_convert_fusion.4
  231.0 31.7 %all_gather.35 = f32[8,128,64]{1,2,0:T(8,128)S(1)} all-gather(f32[1,128,64]{1,2,0:T(8,128)S(1)} %bitcast.83), channel_id=1, replica_groups=mesh['section'=4,'tp'=8] {'tp'}, dimensions={0}, use_global_device_ids=true | all-gather | bytes 294912 | tf_op jit(solution)/shard_map/while/body/eval_jaxpr/all_gather | solution.py:13
  264.9 2.8 all-gather.5.cloned.1.call-done
  267.7 4.0 add_convert_fusion.5
  273.1 1.9 collective-permute-done
  276.7 40.0 %all-gather.3.cloned.1.call-done = bf16[128,4096]{1,0:T(8,128)(2,1)} async-done(((bf16[128,512]{1,0:T(8,128)(2,1)}), bf16[128,4096]{1,0:T(8,128)(2,1)}) %all-gather.3.cloned.1.call-update) | async-done | bytes 1048592 | tf_op jit(solution)/shard_map/while/body/eval_jaxpr/all_gather | solution.py:75
  316.7 4.7 add_convert_fusion.4
  324.5 31.7 %all_gather.35 = f32[8,128,64]{1,2,0:T(8,128)S(1)} all-gather(f32[1,128,64]{1,2,0:T(8,128)S(1)} %bitcast.83), channel_id=1, replica_groups=mesh['section'=4,'tp'=8] {'tp'}, dimensions={0}, use_global_device_ids=true | all-gather | bytes 294912 | tf_op jit(solution)/shard_map/while/body/eval_jaxpr/all_gather | solution.py:13
  358.4 2.8 all-gather.5.cloned.1.call-done
  361.2 4.0 add_convert_fusion.5
  366.6 1.9 collective-permute-done
  370.2 40.0 %all-gather.3.cloned.1.call-done = bf16[128,4096]{1,0:T(8,128)(2,1)} async-done(((bf16[128,512]{1,0:T(8,128)(2,1)}), bf16[128,4096]{1,0:T(8,128)(2,1)}) %all-gather.3.cloned.1.call-update) | async-done | bytes 1048592 | tf_op jit(solution)/shard_map/while/body/eval_jaxpr/all_gather | solution.py:75
  410.2 4.7 add_convert_fusion.4
  418.0 31.7 %all_gather.35 = f32[8,128,64]{1,2,0:T(8,128)S(1)} all-gather(f32[1,128,64]{1,2,0:T(8,128)S(1)} %bitcast.83), channel_id=1, replica_groups=mesh['section'=4,'tp'=8] {'tp'}, dimensions={0}, use_global_device_ids=true | all-gather | bytes 294912 | tf_op jit(solution)/shard_map/while/body/eval_jaxpr/all_gather | solution.py:13
  451.9 2.8 all-gather.5.cloned.1.call-done
  454.7 4.0 add_convert_fusion.5
  460.1 1.9 collective-permute-done
  463.7 40.0 %all-gather.3.cloned.1.call-done = bf16[128,4096]{1,0:T(8,128)(2,1)} async-done(((bf16[128,512]{1,0:T(8,128)(2,1)}), bf16[128,4096]{1,0:T(8,128)(2,1)}) %all-gather.3.cloned.1.call-update) | async-done | bytes 1048592 | tf_op jit(solution)/shard_map/while/body/eval_jaxpr/all_gather | solution.py:75
  503.7 4.7 add_convert_fusion.4
  511.5 31.7 %all_gather.35 = f32[8,128,64]{1,2,0:T(8,128)S(1)} all-gather(f32[1,128,64]{1,2,0:T(8,128)S(1)} %bitcast.83), channel_id=1, replica_groups=mesh['section'=4,'tp'=8] {'tp'}, dimensions={0}, use_global_device_ids=true | all-gather | bytes 294912 | tf_op jit(solution)/shard_map/while/body/eval_jaxpr/all_gather | solution.py:13
  545.4 2.8 all-gather.5.cloned.1.call-done
  548.2 4.0 add_convert_fusion.5
  553.6 1.9 collective-permute-done
  557.2 40.0 %all-gather.3.cloned.1.call-done = bf16[128,4096]{1,0:T(8,128)(2,1)} async-done(((bf16[128,512]{1,0:T(8,128)(2,1)}), bf16[128,4096]{1,0:T(8,128)(2,1)}) %all-gather.3.cloned.1.call-update) | async-done | bytes 1048592 | tf_op jit(solution)/shard_map/while/body/eval_jaxpr/all_gather | solution.py:75
  597.2 4.7 add_convert_fusion.4
  605.0 31.7 %all_gather.35 = f32[8,128,64]{1,2,0:T(8,128)S(1)} all-gather(f32[1,128,64]{1,2,0:T(8,128)S(1)} %bitcast.83), channel_id=1, replica_groups=mesh['section'=4,'tp'=8] {'tp'}, dimensions={0}, use_global_device_ids=true | all-gather | bytes 294912 | tf_op jit(solution)/shard_map/while/body/eval_jaxpr/all_gather | solution.py:13
  638.9 2.8 all-gather.5.cloned.1.call-done
  641.7 4.0 add_convert_fusion.5
  647.1 1.9 collective-permute-done
  650.7 40.0 %all-gather.3.cloned.1.call-done = bf16[128,4096]{1,0:T(8,128)(2,1)} async-done(((bf16[128,512]{1,0:T(8,128)(2,1)}), bf16[128,4096]{1,0:T(8,128)(2,1)}) %all-gather.3.cloned.1.call-update) | async-done | bytes 1048592 | tf_op jit(solution)/shard_map/while/body/eval_jaxpr/all_gather | solution.py:75
  690.7 4.7 add_convert_fusion.4
  698.5 31.7 %all_gather.35 = f32[8,128,64]{1,2,0:T(8,128)S(1)} all-gather(f32[1,128,64]{1,2,0:T(8,128)S(1)} %bitcast.83), channel_id=1, replica_groups=mesh['section'=4,'tp'=8] {'tp'}, dimensions={0}, use_global_device_ids=true | all-gather | bytes 294912 | tf_op jit(solution)/shard_map/while/body/eval_jaxpr/all_gather | solution.py:13
  732.4 2.8 all-gather.5.cloned.1.call-done
  735.2 4.0 add_convert_fusion.5
  739.7 6.2 psum.15
  (136 shorter events, 56.2 us)
Async XLA Ops:
  6.5 732.7 %copy-start = (bf16[2,64,2048]{2,1,0:T(8,128)(2,1)S(1)}, bf16[2,64,2048]{2,1,0:T(8,128)(2,1)}, u32[]{:S(2)}) copy-start(bf16[2,64,2048]{2,1,0:T(8,128)(2,1)} %param.13) | copy-start | bytes 1572868
  6.5 77.9 %all-reduce.2.cloned.1.call-start = ((), (), s32[]{:S(2)}) async-start(), calls=%async_computation | async-start | bytes 524288 | tf_op jit(solution)/shard_map/psum | solution.py:53
  9.2 75.2 %copy-start.3 = (bf16[2,512,32]{1,2,0:T(8,128)(2,1)S(1)}, bf16[2,512,32]{1,2,0:T(8,128)(2,1)}, u32[]{:S(2)}) copy-start(bf16[2,512,32]{1,2,0:T(8,128)(2,1)} %param.12) | copy-start | bytes 196612
  9.2 75.2 %copy-start.4 = (s32[4]{0:T(128)S(1)}, s32[4]{0:T(128)}, u32[]{:S(2)}) copy-start(s32[4]{0:T(128)} %param.15) | copy-start | bytes 52
  84.5 45.3 %all-gather.3.cloned.1.call-start = ((), (), s32[]{:S(2)}) async-start(), calls=%async_computation.1 | async-start | bytes 1179648 | tf_op jit(solution)/shard_map/while/body/eval_jaxpr/all_gather | solution.py:75
  84.5 3.2 collective-permute-start
  89.3 84.8 %all-gather.5.cloned.1.call-start = ((), (), s32[]{:S(2)}) async-start(), calls=%async_computation.2 | async-start | bytes 1179648 | tf_op jit(solution)/shard_map/while/body/eval_jaxpr/all_gather | solution.py:79
  129.7 6.7 copy-start.1
  169.2 4.9 copy-start.2
  178.2 45.0 %all-gather.3.cloned.1.call-start = ((), (), s32[]{:S(2)}) async-start(), calls=%async_computation.1 | async-start | bytes 1179648 | tf_op jit(solution)/shard_map/while/body/eval_jaxpr/all_gather | solution.py:75
  178.3 3.2 collective-permute-start
  183.2 84.5 %all-gather.5.cloned.1.call-start = ((), (), s32[]{:S(2)}) async-start(), calls=%async_computation.2 | async-start | bytes 1179648 | tf_op jit(solution)/shard_map/while/body/eval_jaxpr/all_gather | solution.py:79
  223.2 6.7 copy-start.1
  262.7 5.0 copy-start.2
  271.7 45.0 %all-gather.3.cloned.1.call-start = ((), (), s32[]{:S(2)}) async-start(), calls=%async_computation.1 | async-start | bytes 1179648 | tf_op jit(solution)/shard_map/while/body/eval_jaxpr/all_gather | solution.py:75
  271.8 3.2 collective-permute-start
  276.7 84.5 %all-gather.5.cloned.1.call-start = ((), (), s32[]{:S(2)}) async-start(), calls=%async_computation.2 | async-start | bytes 1179648 | tf_op jit(solution)/shard_map/while/body/eval_jaxpr/all_gather | solution.py:79
  316.7 6.7 copy-start.1
  356.2 5.0 copy-start.2
  365.2 45.0 %all-gather.3.cloned.1.call-start = ((), (), s32[]{:S(2)}) async-start(), calls=%async_computation.1 | async-start | bytes 1179648 | tf_op jit(solution)/shard_map/while/body/eval_jaxpr/all_gather | solution.py:75
  365.3 3.2 collective-permute-start
  370.2 84.5 %all-gather.5.cloned.1.call-start = ((), (), s32[]{:S(2)}) async-start(), calls=%async_computation.2 | async-start | bytes 1179648 | tf_op jit(solution)/shard_map/while/body/eval_jaxpr/all_gather | solution.py:79
  410.2 6.7 copy-start.1
  449.7 5.0 copy-start.2
  458.7 45.0 %all-gather.3.cloned.1.call-start = ((), (), s32[]{:S(2)}) async-start(), calls=%async_computation.1 | async-start | bytes 1179648 | tf_op jit(solution)/shard_map/while/body/eval_jaxpr/all_gather | solution.py:75
  458.8 3.2 collective-permute-start
  463.7 84.5 %all-gather.5.cloned.1.call-start = ((), (), s32[]{:S(2)}) async-start(), calls=%async_computation.2 | async-start | bytes 1179648 | tf_op jit(solution)/shard_map/while/body/eval_jaxpr/all_gather | solution.py:79
  503.7 6.7 copy-start.1
  543.2 5.0 copy-start.2
  552.2 45.0 %all-gather.3.cloned.1.call-start = ((), (), s32[]{:S(2)}) async-start(), calls=%async_computation.1 | async-start | bytes 1179648 | tf_op jit(solution)/shard_map/while/body/eval_jaxpr/all_gather | solution.py:75
  552.3 3.2 collective-permute-start
  557.2 84.5 %all-gather.5.cloned.1.call-start = ((), (), s32[]{:S(2)}) async-start(), calls=%async_computation.2 | async-start | bytes 1179648 | tf_op jit(solution)/shard_map/while/body/eval_jaxpr/all_gather | solution.py:79
  597.2 6.7 copy-start.1
  636.7 5.0 copy-start.2
  645.7 45.0 %all-gather.3.cloned.1.call-start = ((), (), s32[]{:S(2)}) async-start(), calls=%async_computation.1 | async-start | bytes 1179648 | tf_op jit(solution)/shard_map/while/body/eval_jaxpr/all_gather | solution.py:75
  645.8 3.2 collective-permute-start
  650.7 84.5 %all-gather.5.cloned.1.call-start = ((), (), s32[]{:S(2)}) async-start(), calls=%async_computation.2 | async-start | bytes 1179648 | tf_op jit(solution)/shard_map/while/body/eval_jaxpr/all_gather | solution.py:79
  690.7 6.7 copy-start.1
  730.2 5.0 copy-start.2
Sparse Core Ops, SparseCore 0:
  10.7 73.7 all-reduce.1
  89.5 40.2 all-gather.2
  134.6 39.5 all-gather.4
  183.3 39.8 all-gather.2
  228.1 39.5 all-gather.4
  276.8 39.8 all-gather.2
  321.6 39.5 all-gather.4
  370.3 39.8 all-gather.2
  415.1 39.5 all-gather.4
  463.8 39.8 all-gather.2
  508.6 39.5 all-gather.4
  557.3 39.8 all-gather.2
  602.1 39.5 all-gather.4
  650.8 39.8 all-gather.2
  695.6 39.5 all-gather.4
